TPU v7x, 128 devices: a whole 4x4x4 slice. The times are simulated.
128 devices in a mesh: outer: 4 (over z), inner: 32 (over x, y, core).
Axes of the slice: x: 4, y: 4, z: 4, core: 2. Of those that a mesh axis runs over, the one named last changes fastest.
Arguments:
- left_four: float32 [524288, 128], P(('outer', 'inner')), may hold values from -6 to 6
- left_three: float32 [524288, 128], P(('outer', 'inner')), may hold values from -6 to 6
- left_two: float32 [524288, 128], P(('outer', 'inner')), may hold values from -6 to 6
- left_one: float32 [524288, 128], P(('outer', 'inner')), may hold values from -6 to 6
- right_four: float32 [524288, 128], P(('outer', 'inner')), may hold values from -0.0008544922 to 0.0008544922
- right_three: float32 [524288, 128], P(('outer', 'inner')), may hold values from -0.00061035156 to 0.00061035156
- right_two: float32 [524288, 128], P(('outer', 'inner')), may hold values from -0.0004272461 to 0.0004272461
- right_one: float32 [524288, 128], P(('outer', 'inner')), may hold values from -0.00030517578 to 0.00030517578
- loads: float32 [524288, 128], P(('outer', 'inner')), may hold values from -6 to 6
Outputs:
- solution: float32 [524288, 128], P(('outer', 'inner'))
All inputs are finite; a program needn't handle non-finite values.
Results may differ from a plain program's by a relative error of at most 0.0003.
Values sent between devices are 32-bit elements; how exact they have to be, the bound alone decides.
A program may use at most 128 MiB of HBM per device.

v0:
```python
import jax
import jax.numpy as jnp
from jax import lax
from jax.sharding import PartitionSpec as P

highest = lax.Precision.HIGHEST


def partner(value, axis, bit):
    mask = 2**bit
    pairs = [(source, source ^ mask) for source in range(lax.axis_size(axis))]
    return lax.ppermute(value, axis, pairs)


def eliminate(system, targets):
    order = system.shape[0]
    augmented = jnp.concatenate([system, targets], axis=1)

    def pivot_step(pivot_index, matrix):
        pivot_row = lax.dynamic_slice_in_dim(matrix, pivot_index, 1, 0)
        pivot_value = lax.dynamic_slice_in_dim(pivot_row, pivot_index, 1, 1)
        pivot_row = pivot_row / pivot_value
        column = lax.dynamic_slice_in_dim(matrix, pivot_index, 1, 1)
        matrix = matrix - column * pivot_row
        return lax.dynamic_update_slice_in_dim(matrix, pivot_row, pivot_index, 0)

    reduced = lax.fori_loop(0, order, pivot_step, augmented)
    return reduced[:, order:]


def coupled_solve(own_sums, sibling, width):
    own_coupling = own_sums[:, :width]
    own_weights = own_sums[:, width:]
    sib_coupling = sibling[:, :width]
    sib_weights = sibling[:, width:]
    identity = jnp.eye(width, dtype=jnp.float32)
    system = identity - jnp.dot(
        sib_coupling, own_coupling, precision=highest, preferred_element_type=jnp.float32
    )
    targets = sib_weights - jnp.dot(
        sib_coupling, own_weights, precision=highest, preferred_element_type=jnp.float32
    )
    return eliminate(system, targets)


def body(
    left_four, left_three, left_two, left_one, right_four, right_three, right_two, right_one, loads
):
    width = left_four.shape[1]
    n_inner = lax.axis_size("inner")
    devices = lax.axis_size("outer") * n_inner
    basis = left_four
    carried = jnp.concatenate([left_three, left_two, left_one, loads], axis=1)
    updated = carried
    for level_number, right_basis in (
        (4, right_four),
        (3, right_three),
        (2, right_two),
        (1, right_one),
    ):
        stacked = jnp.concatenate([basis, carried], axis=1)
        own_sums = jnp.einsum(
            "nk,nc->kc", right_basis, stacked, precision=highest, preferred_element_type=jnp.float32
        )
        span_devices = devices // 2**level_number
        span_bits = span_devices.bit_length() - 1
        for which_bit in range(span_bits):
            own_sums = own_sums + partner(own_sums, ("outer", "inner"), which_bit)
        sibling = partner(own_sums, ("outer", "inner"), span_bits)
        coefficients = coupled_solve(own_sums, sibling, width)
        updated = stacked[:, width:] - jnp.dot(
            basis, coefficients, precision=highest, preferred_element_type=jnp.float32
        )
        basis = updated[:, :width]
        carried = updated[:, width:]
    return updated


def solution(mesh):
    return jax.shard_map(
        body,
        mesh=mesh,
        in_specs=(
            P(("outer", "inner"), None),
            P(("outer", "inner"), None),
            P(("outer", "inner"), None),
            P(("outer", "inner"), None),
            P(("outer", "inner"), None),
            P(("outer", "inner"), None),
            P(("outer", "inner"), None),
            P(("outer", "inner"), None),
            P(("outer", "inner"), None),
        ),
        out_specs=P(("outer", "inner"), None),
        check_vma=False,
    )
```

profile of v0, /device:TPU:1, one launch (start us, length us, event | category | flops | bytes accessed | tf_op | source)
XLA Modules:
  0.0 1054.7 jit_solution(4420288552922769823)
XLA Ops:
  4.9 16.8 %convolution_bitcast_fusion = f32[128,640]{0,1:T(8,128)S(1)} fusion(f32[4096,640]{1,0:T(8,128)S(1)} %constant_dynamic-update-slice_fusion, f32[4096,128]{1,0:T(8,128)S(1)} %copy-done), kind=kOutput, calls=%fused_computation.19 | convolution fusion | flops 4026531840 | bytes 12910592 | tf_op jit(solution)/shard_map/nk,nc->kc/dot_general | solution.py:62
  26.0 7.5 collective-permute-done.1
  33.5 3.1 collective-permute-start.2
  36.6 6.6 collective-permute-done.2
  46.5 3.1 copy.31
  55.0 215.8 %while.52 = (s32[]{:T(128)}, f32[128,640]{1,0:T(8,128)S(1)}, s32[]{:T(128)}, s32[]{:T(128)}, s32[]{:T(128)}, /*index=5*/s32[]{:T(128)}) while((s32[]{:T(128)}, f32[128,640]{1,0:T(8,128)S(1)}, s32[]{:T(128)}, s32[]{:T(128)}, s32[]{:T(128)}, /*index=5*/s32[]{:T(128)}) %tuple.111), condition=%wide.region_1.0_spmd, body=%wide.region_0.0_spmd.sunk | while | flops 164484 | bytes 672385 | solution.py:27
  270.9 12.9 %maximum_subtract_fusion = f32[4096,512]{0,1:T(8,128)S(1)} fusion(f32[4096,128]{0,1:T(8,128)} %copy.33, f32[4096,128]{0,1:T(8,128)} %copy.32, f32[4096,128]{0,1:T(8,128)} %copy.31, f32[4096,128]{0,1:T(8,128)} %copy.30, f32[4096,128]{1,0:T(8,128)} %param.17, f32[128,640]{1,0:T(8,128)S(1)} %get-tuple-element.201), kind=kOutput, calls=%fused_computation.12 | convolution fusion | flops 3229614080 | bytes 19136512 | tf_op jit(solution)/shard_map/dot_general | solution.py:71
  283.8 6.7 convolution_bitcast_fusion.1
  295.5 6.2 collective-permute-done.5
  304.7 5.2 collective-permute-done.6
  310.2 5.6 collective-permute-done.7
  318.4 4.3 collective-permute-done.8
  323.4 198.7 %while.53 = (s32[]{:T(128)}, f32[128,512]{1,0:T(8,128)S(1)}, s32[]{:T(128)}, s32[]{:T(128)}, s32[]{:T(128)}, /*index=5*/s32[]{:T(128)}) while((s32[]{:T(128)}, f32[128,512]{1,0:T(8,128)S(1)}, s32[]{:T(128)}, s32[]{:T(128)}, s32[]{:T(128)}, /*index=5*/s32[]{:T(128)}) %tuple.114), condition=%wide.region_3.0_spmd, body=%wide.region_2.0_spmd.sunk | while | flops 131588 | bytes 536193 | solution.py:27
  522.1 8.4 slice_subtract_fusion
  530.5 5.1 convolution_bitcast_fusion.2
  535.6 4.2 collective-permute-start.9
  542.2 4.8 collective-permute-done.10
  547.1 3.0 collective-permute-start.11
  550.1 3.8 collective-permute-done.11
  554.2 4.3 collective-permute-done.12
  561.1 3.6 collective-permute-done.13
  566.4 3.1 collective-permute-done.14
  570.1 211.1 %while.54 = (s32[]{:T(128)}, f32[128,384]{1,0:T(8,128)S(1)}, s32[]{:T(128)}, s32[]{:T(128)}, s32[]{:T(128)}, /*index=5*/s32[]{:T(128)}) while((s32[]{:T(128)}, f32[128,384]{1,0:T(8,128)S(1)}, s32[]{:T(128)}, s32[]{:T(128)}, s32[]{:T(128)}, /*index=5*/s32[]{:T(128)}) %tuple.117), condition=%wide.region_5.0_spmd, body=%wide.region_4.0_spmd.sunk | while | flops 98692 | bytes 404097 | solution.py:27
  781.2 6.5 convolution_subtract_fusion
  787.8 3.5 convolution_bitcast_fusion.3
  791.3 5.4 collective-permute-start.15
  799.0 3.4 collective-permute-done.16
  808.2 3.6 collective-permute-done.18
  814.5 3.1 collective-permute-done.19
  821.7 3.5 collective-permute-start.21
  828.1 217.8 %while.55 = (s32[]{:T(128)}, f32[128,256]{1,0:T(8,128)S(1)}, s32[]{:T(128)}, s32[]{:T(128)}, s32[]{:T(128)}, /*index=5*/s32[]{:T(128)}) while((s32[]{:T(128)}, f32[128,256]{1,0:T(8,128)S(1)}, s32[]{:T(128)}, s32[]{:T(128)}, s32[]{:T(128)}, /*index=5*/s32[]{:T(128)}) %tuple.120), condition=%wide.region_7.0_spmd, body=%wide.region_6.0_spmd.sunk | while | flops 65796 | bytes 268929 | solution.py:27
  1046.0 5.7 convolution_subtract_fusion.1
  (2656 shorter events, 877.3 us)
Async XLA Ops:
  0.0 4.9 copy-start
  21.7 22.9 %copy-start.6 = (f32[4096,128]{1,0:T(8,128)S(1)}, f32[4096,128]{1,0:T(8,128)}, u32[]{:S(2)}) copy-start(f32[4096,128]{1,0:T(8,128)} %param.18) | copy-start | bytes 6291460
  21.7 2.7 collective-permute-start
  24.5 9.0 collective-permute-start.1
  33.5 9.7 collective-permute-start.2
  43.3 10.9 %collective-permute-start.3 = (f32[128,640]{0,1:T(8,128)S(1)}, f32[128,640]{0,1:T(8,128)S(1)}, u32[]{:S(2)}, u32[]{:S(2)}) collective-permute-start(f32[128,640]{0,1:T(8,128)S(1)} %add.192), channel_id=1, source_target_pairs={{0,8},{1,9},{2,10},{3,11},{4,12},{5,13},{6,14},{7,15},{8,0},{9,1},... | collective-permute-start | bytes 983048 | tf_op jit(solution)/shard_map/ppermute | solution.py:12
  46.4 3.1 copy-start.9
  270.9 12.9 %copy-start.11 = (f32[4096,128]{1,0:T(8,128)S(1)}, f32[4096,128]{1,0:T(8,128)}, u32[]{:S(2)}) copy-start(f32[4096,128]{1,0:T(8,128)} %param.22) | copy-start | bytes 6291460
  283.8 6.7 copy-start.2
  290.5 3.6 collective-permute-start.4
  294.1 7.6 collective-permute-start.5
  301.7 8.2 collective-permute-start.6
  310.0 5.9 collective-permute-start.7
  315.9 6.8 collective-permute-start.8
  522.1 8.4 copy-start.13
  530.5 5.1 copy-start.3
  535.6 5.2 collective-permute-start.9
  540.9 6.2 collective-permute-start.10
  547.1 6.8 collective-permute-start.11
  553.9 4.6 collective-permute-start.12
  558.5 6.2 collective-permute-start.13
  564.7 4.8 collective-permute-start.14
  781.2 6.6 copy-start.12
  787.8 33.9 %copy-start.4 = (f32[4096,256]{0,1:T(8,128)}, f32[4096,256]{0,1:T(8,128)S(1)}, u32[]{:S(2)}) copy-start(f32[4096,256]{0,1:T(8,128)S(1)} %convolution_subtract_fusion) | copy-start | bytes 12582916
  791.3 6.4 collective-permute-start.15
  797.7 4.8 collective-permute-start.16
  802.5 5.4 collective-permute-start.17
  807.9 3.9 collective-permute-start.18
  811.8 5.8 collective-permute-start.19
  817.6 4.1 collective-permute-start.20
  821.7 5.9 collective-permute-start.21
  1045.9 8.6 copy-start.1
  (4 other events, 8.9 us)
where the time goes:
time: 1070 us; the launch traced here: 1050 us
  local copies, waits for them, and re-layouts  453 us (42%)
  other arithmetic  385 us (36%)
  waiting for transfers between devices  76.8 us (7%)
  matrix products  67.5 us (6%)
  starting transfers between devices  47.9 us (4%)
  loops' own time  23.9 us (2%)
    div x512, other arithmetic, pivot_step(): pivot_row = pivot_row / pivot_value  328 us
    dynamic_slice x512, local copies, waits for them, and re-layouts, pivot_step(): pivot_value = lax.dynamic_slice_in_dim(pivot_row, pivot_index, 1, 1)  315 us
    dynamic_slice x512, local copies, waits for them, and re-layouts, pivot_step(): column = lax.dynamic_slice_in_dim(matrix, pivot_index, 1, 1)  90.5 us
    ppermute x22, waiting for transfers between devices, partner(): return lax.ppermute(value, axis, pairs)  76.8 us
    sub x512, other arithmetic, pivot_step(): matrix = matrix - column * pivot_row  56.8 us
    ppermute x22, starting transfers between devices, partner(): return lax.ppermute(value, axis, pairs)  47.9 us
    dot_general x4, matrix products, body(): jnp.dot(basis, coefficients, precision=highest, preferred_element_type=jn...  33.5 us
    dot_general x4, matrix products, body(): jnp.einsum('nk,nc->kc', right_basis, stacked, precision=highest, preferre...  32 us
  transfers between devices with their start and end apart: 22, of which 21 were waited for; matrix products, arithmetic and copies ran while one was open for 1% of the time, Pallas kernels for 0%

commit v1 on v0

v1 whole, which is shorter than its diff:
```python
import functools

import jax
import jax.numpy as jnp
from jax import lax
from jax.experimental import pallas as pl
from jax.experimental.pallas import tpu as pltpu
from jax.sharding import PartitionSpec as P

W = 128
HIGH = lax.Precision.HIGH
HIGHEST = lax.Precision.HIGHEST
MESH = pl.DeviceIdType.MESH


def dot(a, b, precision=HIGHEST):
    return jnp.dot(a, b, precision=precision, preferred_element_type=jnp.float32)


def split(v):
    high = v.astype(jnp.bfloat16)
    low = (v - high.astype(jnp.float32)).astype(jnp.bfloat16)
    return high, low


def products_kernel(l4, l3, l2, l1, x, r4, r3, r2, r1, out, acc):
    step = pl.program_id(0)

    @pl.when(step == 0)
    def _():
        acc[...] = jnp.zeros_like(acc)

    rights = jnp.concatenate([r4[...], r3[...], r2[...], r1[...]], axis=1)
    r_high, r_low = split(rights)
    a_high, a_low = [], []
    for ref in (l4, l3, l2, l1, x):
        high, low = split(ref[...].T)
        a_high.append(high)
        a_low.append(low)
    a_high = jnp.concatenate(a_high, axis=0)
    a_low = jnp.concatenate(a_low, axis=0)
    one = functools.partial(jnp.dot, preferred_element_type=jnp.float32)
    acc[...] += one(a_high, r_high) + one(a_high, r_low) + one(a_low, r_high)

    @pl.when(step == pl.num_programs(0) - 1)
    def _():
        for core in range(2):
            for y in range(4):
                piece = y * 2 + core
                for block in range(5):
                    out[core, y, 16 * block : 16 * block + 16, :] = acc[
                        W * block + 16 * piece : W * block + 16 * piece + 16, :
                    ]


def products(lefts, rights, tile=512):
    rows = lefts[0].shape[0]
    spec = pl.BlockSpec((tile, W), lambda i: (i, 0))
    return pl.pallas_call(
        products_kernel,
        grid=(rows // tile,),
        out_shape=jax.ShapeDtypeStruct((2, 4, 80, 512), jnp.float32),
        in_specs=[spec] * 9,
        out_specs=pl.BlockSpec((2, 4, 80, 512), lambda i: (0, 0, 0, 0)),
        scratch_shapes=[pltpu.VMEM((640, 512), jnp.float32)],
        name="products",
    )(*lefts, *rights)


def inverse(matrix):
    tiles = [matrix[8 * i : 8 * i + 8, :] for i in range(16)]
    lane = lax.broadcasted_iota(jnp.int32, (8, W), 1)
    sub = lax.broadcasted_iota(jnp.int32, (8, W), 0)

    def block_step(block, tiles):
        first = block * 8
        in_block = (lane >= first) & (lane < first + 8)
        on_diag = lane == first + sub

        def column(tile, i):
            index = jnp.zeros((8, W), jnp.int32) + (first + i)
            return jnp.take_along_axis(tile, index, axis=1, mode="promise_in_bounds")

        pivot_tile = tiles[0]
        cols = [column(pivot_tile, i) for i in range(8)]
        panel = jnp.where(in_block, jnp.where(on_diag, 1.0, 0.0), pivot_tile)
        for i in range(8):
            inv = 1.0 / jnp.broadcast_to(cols[i][i : i + 1, :], (8, W))
            here = sub == i
            row = jnp.broadcast_to(panel[i : i + 1, :], (8, W)) * inv
            panel = jnp.where(here, row, panel - cols[i] * row)
            for j in range(i + 1, 8):
                row = jnp.broadcast_to(cols[j][i : i + 1, :], (8, W)) * inv
                cols[j] = jnp.where(here, row, cols[j] - cols[i] * row)
        rows = [jnp.broadcast_to(panel[i : i + 1, :], (8, W)) for i in range(8)]
        updated = []
        for tile in tiles[1:]:
            total = column(tile, 0) * rows[0]
            for i in range(1, 8):
                total = total + column(tile, i) * rows[i]
            updated.append(jnp.where(in_block, 0.0, tile) - total)
        return tuple(updated) + (panel,)

    tiles = lax.fori_loop(0, 16, block_step, tuple(tiles))
    return jnp.concatenate(tiles, axis=0)


def tree_kernel(h, coef, half, rx1, rx2, own, rest, gat, gatx, us, sems):
    z = lax.axis_index("outer")
    inner = lax.axis_index("inner")
    x = inner // 8
    y = lax.rem(inner, 8) // 2
    core = lax.rem(inner, 2)
    mine = y * 2 + core

    def device(dz_to, x_to, dy, dc):
        y_to = lax.rem(y + dy, 4)
        c_to = lax.rem(core + dc, 2)
        return (dz_to, x_to * 8 + y_to * 2 + c_to)

    partners = (
        (z, x + 1 - 2 * lax.rem(x, 2)),
        (z, lax.rem(x + 2, 4)),
        (z + 1 - 2 * lax.rem(z, 2), x),
        (lax.rem(z + 2, 4), x),
    )
    around = [(dy, dc) for dy in range(4) for dc in range(2)]
    peers = [(z, x, dy, dc) for dy, dc in around if (dy, dc) != (0, 0)]
    for zp, xp in partners:
        peers += [(zp, xp, dy, dc) for dy, dc in around]
    barrier = pltpu.get_barrier_semaphore()
    for peer in peers:
        pl.semaphore_signal(barrier, inc=1, device_id=device(*peer), device_id_type=MESH)
    pl.semaphore_wait(barrier, len(peers))

    count = [0]
    started = []

    def send(src, dst, to):
        k = count[0]
        count[0] += 1
        copy = pltpu.make_async_remote_copy(
            src_ref=src, dst_ref=dst, send_sem=sems.at[0, k], recv_sem=sems.at[1, k],
            device_id=device(*to), device_id_type=MESH,
        )
        copy.start()
        started.append(copy)
        return copy

    def receive(copies):
        for copy in copies:
            copy.wait_recv()

    first = send(h.at[1 - core], rx1, (z, x, 0, 1))
    receive([first])
    half[...] = h[core] + rx1[...]
    copies = []
    for dy in (1, 2, 3):
        copies.append(send(half.at[lax.rem(y + dy, 4)], rx2.at[dy - 1], (z, x, dy, 0)))
    receive(copies)
    own[0][...] = half[y] + rx2[0] + rx2[1] + rx2[2]

    eye = jnp.where(
        lax.broadcasted_iota(jnp.int32, (W, W), 0) == lax.broadcasted_iota(jnp.int32, (W, W), 1), 1.0, 0.0
    )
    spread = []
    for level in range(4):
        lanes = 4 - level
        rows = 16 * lanes
        zp, xp = partners[level]
        mat, gather = own[level], gat[level]
        at = pl.ds(pl.multiple_of(mine * 16, 16), 16)
        pivots, others, x_rows = [], [], []
        for side in range(2):
            zt, xt = ((z, x), (zp, xp))[side]
            for dy, dc in around:
                if side == 0 and (dy, dc) == (0, 0):
                    continue
                to = (zt, xt, dy, dc)
                pivots.append(send(mat.at[0:16, 0:W], gather.at[side, at, 0:W], to))
                if level == 3:
                    x_rows.append(send(mat.at[16:32, :], gatx.at[side, at, :], to))
        if level < 3:
            partner_copy = send(mat.at[16 : 16 + rows, :], rest[level], (zp, xp, 0, 0))
            for side in range(2):
                zt, xt = ((z, x), (zp, xp))[side]
                for dy, dc in around:
                    if side == 0 and (dy, dc) == (0, 0):
                        continue
                    to = (zt, xt, dy, dc)
                    others.append(send(mat.at[0:16, W:], gather.at[side, at, W:], to))
        gather[0, at, :] = mat[0:16, :]
        if level == 3:
            gatx[0, at, :] = mat[16:32, :]
        receive(pivots)
        p_own = gather[0, :, 0:W]
        p_sib = gather[1, :, 0:W]
        inv = inverse(eye - dot(p_own, p_sib))
        if level < 3:
            receive([partner_copy])
            w_own = mat[16 : 16 + rows, 0:W]
            w_sib = rest[level][:, 0:W]
        else:
            receive(x_rows)
            w_own = gatx[0]
            w_sib = gatx[1]
        u_own = dot(w_sib - dot(w_own, p_sib), inv)
        if level == 3:
            y_one = u_own
            break
        us[level][mine] = u_own
        copies = []
        for dy, dc in around[1:]:
            copies.append(send(us[level].at[mine], us[level].at[mine], (z, x, dy, dc)))
        spread.append(copies)
        u_sib = w_own - dot(u_own, p_own)
        receive(others)
        own[level + 1][...] = (
            mat[16 : 16 + rows, W:]
            + rest[level][:, W:]
            - dot(u_own, gather[0, :, W:])
            - dot(u_sib, gather[1, :, W:])
        )

    for copies in spread:
        receive(copies)
    u4 = [us[0][:, 16 * b : 16 * b + 16, :].reshape(W, W) for b in range(4)]
    u3 = [us[1][:, 16 * b : 16 * b + 16, :].reshape(W, W) for b in range(3)]
    u2 = [us[2][:, 16 * b : 16 * b + 16, :].reshape(W, W) for b in range(2)]
    y_two = u2[1] - dot(y_one, u2[0])
    y_three = u3[2] - dot(y_one, u3[1]) - dot(y_two, u3[0])
    y_four = u4[3] - dot(y_one, u4[2]) - dot(y_two, u4[1]) - dot(y_three, u4[0])
    coef[0] = y_four
    coef[1] = y_three
    coef[2] = y_two
    coef[3] = y_one
    for copy in started:
        copy.wait_send()


def tree(sums):
    f32 = jnp.float32
    vmem = pl.BlockSpec(memory_space=pltpu.VMEM)
    n_copies = 4 + 4 * 15 + 15 + 3 + 3 * 15 + 3 * 7
    return pl.pallas_call(
        tree_kernel,
        out_shape=jax.ShapeDtypeStruct((4, W, W), f32),
        in_specs=[vmem],
        out_specs=vmem,
        scratch_shapes=[
            pltpu.VMEM((4, 80, 512), f32),
            pltpu.VMEM((4, 80, 512), f32),
            pltpu.VMEM((3, 80, 512), f32),
            [pltpu.VMEM((16 * (5 - k), W * (4 - k)), f32) for k in range(4)],
            [pltpu.VMEM((16 * (4 - k), W * (4 - k)), f32) for k in range(3)],
            [pltpu.VMEM((2, W, W * (4 - k)), f32) for k in range(4)],
            pltpu.VMEM((2, W, W), f32),
            [pltpu.VMEM((8, 16 * (4 - k), W), f32) for k in range(3)],
            pltpu.SemaphoreType.DMA((2, n_copies)),
        ],
        compiler_params=pltpu.CompilerParams(collective_id=0, has_side_effects=True),
        name="tree",
    )(sums)


def update_kernel(l4, l3, l2, l1, x, coef, out):
    total = x[...]
    for index, ref in enumerate((l4, l3, l2, l1)):
        total = total - lax.dot_general(
            ref[...], coef[index], (((1,), (1,)), ((), ())), precision=HIGH, preferred_element_type=jnp.float32
        )
    out[...] = total


def update(lefts, coef, tile=512):
    rows = lefts[0].shape[0]
    spec = pl.BlockSpec((tile, W), lambda i: (i, 0))
    return pl.pallas_call(
        update_kernel,
        grid=(rows // tile,),
        out_shape=jax.ShapeDtypeStruct((rows, W), jnp.float32),
        in_specs=[spec] * 5 + [pl.BlockSpec((4, W, W), lambda i: (0, 0, 0))],
        out_specs=spec,
        name="update",
    )(*lefts, coef)


def body(l4, l3, l2, l1, r4, r3, r2, r1, x):
    lefts = (l4, l3, l2, l1, x)
    sums = products(lefts, (r4, r3, r2, r1))
    coef = tree(sums)
    return update(lefts, coef)


def solution(mesh):
    spec = P(("outer", "inner"), None)
    return jax.shard_map(body, mesh=mesh, in_specs=(spec,) * 9, out_specs=spec, check_vma=False)
```

time: 1070 us -> 107 us (0.10); the launches traced: 1050 us -> 106 us
  local copies, waits for them, and re-layouts: 453 us -> 0 us
  other arithmetic: 385 us -> 0 us
  Pallas kernels: 0 us -> 106 us
  waiting for transfers between devices: 76.8 us -> 0 us
  matrix products: 67.5 us -> 0 us
  starting transfers between devices: 47.9 us -> 0 us
  loops' own time: 23.9 us -> 0 us
    dynamic_slice x1024 -> x0, local copies, waits for them, and re-layouts: 405 us -> none  [the longest x512 315 us: pivot_step(): pivot_value = lax.dynamic_slice_in_dim(pivot_row, pivot_index, 1, 1)]
    div x512 -> x0, other arithmetic: 328 us -> none  [pivot_step(): pivot_row = pivot_row / pivot_value]
    pallas_call x0 -> x3, Pallas kernels: none -> 106 us  [the longest x1 82.8 us: tree(): pl.pallas_call(tree_kernel, out_shape=jax.ShapeDtypeStruct((4, W, W), f32...]
    ppermute x22 -> x0, waiting for transfers between devices: 76.8 us -> none  [partner(): return lax.ppermute(value, axis, pairs)]
    dot_general x16 -> x0, matrix products: 67.5 us -> none  [the longest x4 33.5 us: body(): jnp.dot(basis, coefficients, precision=highest, preferred_element_type=jn...]
    sub x512 -> x0, other arithmetic: 56.8 us -> none  [pivot_step(): matrix = matrix - column * pivot_row]
    ppermute x22 -> x0, starting transfers between devices: 47.9 us -> none  [partner(): return lax.ppermute(value, axis, pairs)]
    dynamic_update_slice x512 -> x0, local copies, waits for them, and re-layouts: 29.9 us -> none  [pivot_step(): return lax.dynamic_update_slice_in_dim(matrix, pivot_row, pivot_index, 0)]
  transfers between devices with their start and end apart: 22 -> 0, of which waited for: 21 -> 0; matrix products, arithmetic and copies ran while one was open for 1% -> 0% of each run, Pallas kernels for 0% -> 0%
where the time goes in v1:
time: 107 us; the launch traced here: 106 us
  Pallas kernels  106 us (99%)
    pallas_call x1, Pallas kernels, tree(): pl.pallas_call(tree_kernel, out_shape=jax.ShapeDtypeStruct((4, W, W), f32...  82.8 us
    pallas_call x1, Pallas kernels, products(): pl.pallas_call(products_kernel, grid=(rows // tile,), out_shape=jax.Shape...  14 us
    pallas_call x1, Pallas kernels, update(): pl.pallas_call(update_kernel, grid=(rows // tile,), out_shape=jax.ShapeDt...  9.67 us

profile of v1, /device:TPU:1, one launch (start us, length us, event | category | flops | bytes accessed | tf_op | source)
XLA Modules:
  0.0 106.4 jit_solution(16794776516704793575)
XLA Ops:
  0.0 14.0 %products.1.h = f32[2,4,80,512]{3,2,1,0:T(8,128)} custom-call(f32[4096,128]{1,0:T(8,128)} %l4.3, f32[4096,128]{1,0:T(8,128)} %l3.3, f32[4096,128]{1,0:T(8,128)} %l2.3, f32[4096,128]{1,0:T(8,128)} %l1.3, f32[4096,128]{1,0:T(8,128)} %x.3, f32[4096,128]{1,0:T(8,128)} %r4.1, f32[4096,128]{1,0:T(8,128)} %r3.1, f32[4096,128]{1,0:T(8,128)} %r2.1, f32[4096,128]{1,0:T(8,128)} %r1.1), custom_call_target="tpu_custom_call" | custom-call | tf_op jit(solution)/shard_map/products/pallas_call | solution.py:59
  14.0 82.8 %tree.1.coef = f32[4,128,128]{2,1,0:T(8,128)} custom-call(f32[2,4,80,512]{3,2,1,0:T(8,128)} %products.1.h), custom_call_target="tpu_custom_call" | custom-call | tf_op jit(solution)/shard_map/tree/pallas_call | solution.py:245
  96.8 9.7 %update.1 = f32[4096,128]{1,0:T(8,128)} custom-call(f32[4096,128]{1,0:T(8,128)} %l4.3, f32[4096,128]{1,0:T(8,128)} %l3.3, f32[4096,128]{1,0:T(8,128)} %l2.3, f32[4096,128]{1,0:T(8,128)} %l1.3, f32[4096,128]{1,0:T(8,128)} %x.3, f32[4,128,128]{2,1,0:T(8,128)} %tree.1.coef), custom_call_target="tpu_custom_call" | custom-call | tf_op jit(solution)/shard_map/update/pallas_call | solution.py:278

commit v2 on v1

v2 whole, which is shorter than its diff:
```python
import functools

import jax
import jax.numpy as jnp
from jax import lax
from jax.experimental import pallas as pl
from jax.experimental.pallas import tpu as pltpu
from jax.sharding import PartitionSpec as P

W = 128
HIGH = lax.Precision.HIGH
HIGHEST = lax.Precision.HIGHEST
MESH = pl.DeviceIdType.MESH


def dot(a, b, precision=HIGHEST):
    return jnp.dot(a, b, precision=precision, preferred_element_type=jnp.float32)


def split(v):
    high = v.astype(jnp.bfloat16)
    low = (v - high.astype(jnp.float32)).astype(jnp.bfloat16)
    return high, low


def inverse(matrix, between):
    tiles = [matrix[8 * i : 8 * i + 8, :] for i in range(16)]
    lane = lax.broadcasted_iota(jnp.int32, (8, W), 1)
    sub = lax.broadcasted_iota(jnp.int32, (8, W), 0)

    def block_step(block, tiles):
        first = block * 8
        in_block = (lane >= first) & (lane < first + 8)
        on_diag = lane == first + sub

        def column(tile, i):
            index = jnp.zeros((8, W), jnp.int32) + (first + i)
            return jnp.take_along_axis(tile, index, axis=1, mode="promise_in_bounds")

        pivot_tile = tiles[0]
        cols = [column(pivot_tile, i) for i in range(8)]
        panel = jnp.where(in_block, jnp.where(on_diag, 1.0, 0.0), pivot_tile)
        for i in range(8):
            inv = 1.0 / jnp.broadcast_to(cols[i][i : i + 1, :], (8, W))
            here = sub == i
            row = jnp.broadcast_to(panel[i : i + 1, :], (8, W)) * inv
            panel = jnp.where(here, row, panel - cols[i] * row)
            for j in range(i + 1, 8):
                row = jnp.broadcast_to(cols[j][i : i + 1, :], (8, W)) * inv
                cols[j] = jnp.where(here, row, cols[j] - cols[i] * row)
        rows = [jnp.broadcast_to(panel[i : i + 1, :], (8, W)) for i in range(8)]
        updated = []
        for tile in tiles[1:]:
            total = column(tile, 0) * rows[0]
            for i in range(1, 8):
                total = total + column(tile, i) * rows[i]
            updated.append(jnp.where(in_block, 0.0, tile) - total)
        return tuple(updated) + (panel,)

    tiles = lax.fori_loop(0, 8, block_step, tuple(tiles))
    between()
    tiles = lax.fori_loop(8, 16, block_step, tiles)
    return jnp.concatenate(tiles, axis=0)


ROWS = 4096
CHUNK = 512
CHUNKS = ROWS // CHUNK


def solve_kernel(
    l4, l3, l2, l1, x_in, r4, r3, r2, r1, out, a_buf, r_buf, r_high, r_low, h, rx1, half, rx2,
    own, rest, gat, gatx, us, load_sems, out_sems, sems,
):
    z = lax.axis_index("outer")
    inner = lax.axis_index("inner")
    x = inner // 8
    y = lax.rem(inner, 8) // 2
    core = lax.rem(inner, 2)
    mine = core * 4 + y

    def device(z_to, x_to, dy, dc):
        y_to = lax.rem(y + dy, 4)
        c_to = lax.rem(core + dc, 2)
        return (z_to, x_to * 8 + y_to * 2 + c_to)

    partners = (
        (z, x + 1 - 2 * lax.rem(x, 2)),
        (z, lax.rem(x + 2, 4)),
        (z + 1 - 2 * lax.rem(z, 2), x),
        (lax.rem(z + 2, 4), x),
    )
    around = [(dy, dc) for dc in range(2) for dy in range(4)]
    peers = [(z, x, dy, dc) for dy, dc in around[1:]]
    for zp, xp in partners:
        peers += [(zp, xp, dy, dc) for dy, dc in around]
    barrier = pltpu.get_barrier_semaphore()
    for peer in peers:
        pl.semaphore_signal(barrier, inc=1, device_id=device(*peer), device_id_type=MESH)

    def load(source, target, k):
        loads = []
        for c in range(CHUNKS):
            rows = pl.ds(c * CHUNK, CHUNK)
            loads.append(pltpu.make_async_copy(source.at[rows, :], target.at[rows, :], load_sems.at[k, c]))
        return loads

    rights = [load(ref, r_buf.at[i], 5 + i) for i, ref in enumerate((r4, r3, r2, r1))]
    lefts = [load(ref, a_buf.at[i], i) for i, ref in enumerate((l4, l3, l2, l1, x_in))]
    for c in range(CHUNKS):
        for loads in rights + lefts[:1]:
            loads[c].start()
    for loads in lefts[1:]:
        for copy in loads:
            copy.start()

    count = [0]
    started = []

    def send(src, dst, to):
        k = count[0]
        count[0] += 1
        copy = pltpu.make_async_remote_copy(
            src_ref=src, dst_ref=dst, send_sem=sems.at[0, k], recv_sem=sems.at[1, k],
            device_id=device(*to), device_id_type=MESH,
        )
        copy.start()
        started.append(copy)
        return copy

    def receive(copies):
        for copy in copies:
            copy.wait_recv()

    one = functools.partial(jnp.dot, preferred_element_type=jnp.float32)

    def product(group, start, size):
        rows = pl.ds(start, size)
        high, low = split(a_buf[group, rows, :].T)
        both = one(jnp.concatenate([high, low], axis=0), r_high[rows, :])
        total = both[:W] + both[W:] + one(high, r_low[rows, :])
        return total.reshape(2, 4, 16, 512)

    mine_rows = pl.ds(pl.multiple_of(mine * 16, 16), 16)
    core_rows = pl.ds(pl.multiple_of(core * 64, 64), 64)
    pivots = [[] for _ in range(4)]
    others = [[] for _ in range(4)]
    nexts = [[] for _ in range(4)]
    rests = [[] for _ in range(4)]

    def send_pivot_rows(level):
        mat, gather = own[level], gat[level]
        zp, xp = partners[level]
        targets = [(z, x, dy, dc) for dy, dc in around[1:]] + [(zp, xp, dy, dc) for dy, dc in around]
        for k, to in enumerate(targets):
            side = 0 if k < 7 else 1
            pivots[level].append(send(mat.at[0:16, 0:W], gather.at[side, mine_rows, 0:W], to))
        gather[0, mine_rows, :] = mat[0:16, :]

    def send_side_rows(level):
        zp, xp = partners[level]
        targets = [(z, x, dy, 0) for dy in (1, 2, 3)] + [(zp, xp, dy, 0) for dy in range(4)]
        for k, to in enumerate(targets):
            side = 0 if k < 3 else 1
            if level < 3:
                copy = send(own[level].at[0:16, W:], gat[level].at[side, mine_rows, W:], to)
            else:
                copy = send(own[3].at[16:32, :], gatx.at[side, mine_rows, :], to)
            others[level].append(copy)
        if level == 3:
            gatx[0, mine_rows, :] = own[3][16:32, :]

    first = [None] * 5
    second = [None] * 5

    def sum_cores(group):
        first[group] = send(h[group].at[1 - core], rx1[group], (z, x, 0, 1))

    def sum_chips(group):
        receive([first[group]])
        half[group][...] = h[group][core] + rx1[group][...]
        second[group] = [
            send(half[group].at[lax.rem(y + dy, 4)], rx2[group].at[dy - 1], (z, x, dy, 0)) for dy in (1, 2, 3)
        ]

    def finish_sum(group):
        receive(second[group])
        rows = slice(16 * group, 16 * group + 16)
        own[0][rows, :] = half[group][y] + rx2[group][0] + rx2[group][1] + rx2[group][2]
        if group == 0:
            send_pivot_rows(0)
            send_side_rows(0)
        else:
            target = rest[0].at[16 * (group - 1) : 16 * group, :]
            copy = send(own[0].at[rows, :], target, partners[0] + (0, 0))
            (nexts if group == 1 else rests)[0].append(copy)

    for c in range(CHUNKS):
        rows = pl.ds(c * CHUNK, CHUNK)
        for i, loads in enumerate(rights):
            loads[c].wait()
            high, low = split(r_buf[i, rows, :])
            r_high[rows, W * i : W * i + W] = high
            r_low[rows, W * i : W * i + W] = low
        lefts[0][c].wait()
        part = product(0, c * CHUNK, CHUNK)
        if c == 0:
            h[0][...] = part
        else:
            h[0][...] += part
    pl.semaphore_wait(barrier, len(peers))
    sum_cores(0)
    for group in range(1, 5):
        for part in range(2):
            for c in range(CHUNKS // 2):
                lefts[group][part * (CHUNKS // 2) + c].wait()
            value = product(group, part * (ROWS // 2), ROWS // 2)
            if part == 0:
                h[group][...] = value
                sum_chips(group - 1)
                if group > 1:
                    finish_sum(group - 2)
            else:
                h[group][...] += value
        sum_cores(group)

    eye = jnp.where(
        lax.broadcasted_iota(jnp.int32, (W, W), 0) == lax.broadcasted_iota(jnp.int32, (W, W), 1), 1.0, 0.0
    )
    forwards = []
    spread = [[] for _ in range(3)]

    def forward(ref):
        forwards.append(send(ref, ref, (z, x, 0, 1)))
        return forwards[-1]

    u_forwards = []
    for level in range(4):
        lanes = 4 - level
        mat, gather = own[level], gat[level]
        if level == 0:
            sum_chips(4)
            finish_sum(3)
        receive(pivots[level])
        p_own = gather[0, :, 0:W]
        p_sib = gather[1, :, 0:W]
        side_forward = []

        def between(level=level, gather=gather, side_forward=side_forward):
            receive(others[level])
            if level < 3:
                side_forward.append(forward(gather.at[:, core_rows, W:]))
            else:
                side_forward.append(forward(gatx.at[:, core_rows, :]))
            if level > 0:
                receive(spread[level - 1])
                u_forwards.append(forward(us[level - 1].at[pl.ds(core * 4, 4)]))

        inv = inverse(eye - dot(p_own, p_sib), between)
        if level == 3:
            receive(side_forward)
            y_one = dot(gatx[1] - dot(gatx[0], p_sib), inv)
            break
        if level == 0:
            finish_sum(4)
        for stage in range(2):
            low, top = (16, 32) if stage == 0 else (32, 16 + 16 * lanes)
            receive((nexts if stage == 0 else rests)[level])
            w_own = mat[low:top, 0:W]
            w_sib = rest[level][low - 16 : top - 16, 0:W]
            u_own = dot(w_sib - dot(w_own, p_sib), inv)
            u_sib = w_own - dot(u_own, p_own)
            us[level][mine, low - 16 : top - 16, :] = u_own
            if stage == 0:
                receive(side_forward)
            own[level + 1][low - 16 : top - 16, :] = (
                mat[low:top, W:]
                + rest[level][low - 16 : top - 16, W:]
                - dot(u_own, gather[0, :, W:])
                - dot(u_sib, gather[1, :, W:])
            )
            if stage == 0:
                send_pivot_rows(level + 1)
                if level < 2:
                    send_side_rows(level + 1)
        partner = partners[level + 1] + (0, 0)
        if level < 2:
            nexts[level + 1].append(send(own[level + 1].at[16:32, :], rest[level + 1].at[0:16, :], partner))
            rests[level + 1].append(send(own[level + 1].at[32:, :], rest[level + 1].at[16:, :], partner))
        else:
            send_side_rows(3)
        for dy in (1, 2, 3):
            spread[level].append(send(us[level].at[mine], us[level].at[mine], (z, x, dy, 0)))

    receive(u_forwards)
    u4 = [us[0][:, 16 * b : 16 * b + 16, :].reshape(W, W) for b in range(4)]
    u3 = [us[1][:, 16 * b : 16 * b + 16, :].reshape(W, W) for b in range(3)]
    u2 = [us[2][:, 16 * b : 16 * b + 16, :].reshape(W, W) for b in range(2)]
    y_two = u2[1] - dot(y_one, u2[0])
    y_three = u3[2] - dot(y_one, u3[1]) - dot(y_two, u3[0])
    y_four = u4[3] - dot(y_one, u4[2]) - dot(y_two, u4[1]) - dot(y_three, u4[0])

    y_high, y_low = split(jnp.concatenate([y_four.T, y_three.T, y_two.T, y_one.T], axis=0))
    y_both = jnp.concatenate([y_high, y_low], axis=1)
    stores = []
    for c in range(CHUNKS):
        rows = pl.ds(c * CHUNK, CHUNK)
        basis = jnp.concatenate([a_buf[i, rows, :] for i in range(4)], axis=1)
        high, low = split(basis)
        both = one(high, y_both)
        a_buf[4, rows, :] = a_buf[4, rows, :] - (both[:, :W] + both[:, W:] + one(low, y_high))
        stores.append(pltpu.make_async_copy(a_buf.at[4, rows, :], out.at[rows, :], out_sems.at[c]))
        stores[-1].start()
    for copy in stores:
        copy.wait()
    for copy in started:
        copy.wait_send()


def body(l4, l3, l2, l1, r4, r3, r2, r1, x):
    f32, bf16 = jnp.float32, jnp.bfloat16
    hbm = pl.BlockSpec(memory_space=pl.ANY)
    n_copies = 5 * 4 + 4 + 4 * 15 + 4 * 7 + 2 * 2 + 4 + 3 * 3 + 3
    return pl.pallas_call(
        solve_kernel,
        out_shape=jax.ShapeDtypeStruct((ROWS, W), f32),
        in_specs=[hbm] * 9,
        out_specs=hbm,
        scratch_shapes=[
            pltpu.VMEM((5, ROWS, W), f32),
            pltpu.VMEM((4, ROWS, W), f32),
            pltpu.VMEM((ROWS, 512), bf16),
            pltpu.VMEM((ROWS, 512), bf16),
            [pltpu.VMEM((2, 4, 16, 512), f32) for _ in range(5)],
            [pltpu.VMEM((4, 16, 512), f32) for _ in range(5)],
            [pltpu.VMEM((4, 16, 512), f32) for _ in range(5)],
            [pltpu.VMEM((3, 16, 512), f32) for _ in range(5)],
            [pltpu.VMEM((16 * (5 - k), W * (4 - k)), f32) for k in range(4)],
            [pltpu.VMEM((16 * (4 - k), W * (4 - k)), f32) for k in range(3)],
            [pltpu.VMEM((2, W, W * (4 - k)), f32) for k in range(4)],
            pltpu.VMEM((2, W, W), f32),
            [pltpu.VMEM((8, 16 * (4 - k), W), f32) for k in range(3)],
            pltpu.SemaphoreType.DMA((9, CHUNKS)),
            pltpu.SemaphoreType.DMA((CHUNKS,)),
            pltpu.SemaphoreType.DMA((2, n_copies)),
        ],
        compiler_params=pltpu.CompilerParams(
            collective_id=0, has_side_effects=True, vmem_limit_bytes=60 * 1024 * 1024
        ),
        name="solve",
    )(l4, l3, l2, l1, x, r4, r3, r2, r1)


def solution(mesh):
    spec = P(("outer", "inner"), None)
    return jax.shard_map(body, mesh=mesh, in_specs=(spec,) * 9, out_specs=spec, check_vma=False)
```

time: 107 us -> 84.3 us (0.79)
  Pallas kernels: 106 us -> 81.1 us
  local copies, waits for them, and re-layouts: 0 us -> 3.05 us
    pallas_call x3 -> x1, Pallas kernels: 106 us -> 81.1 us  [body(): pl.pallas_call(solve_kernel, out_shape=jax.ShapeDtypeStruct((ROWS, W), f3...]
    unnamed x0 -> x1, local copies, waits for them, and re-layouts: none -> 3.05 us
where the time goes in v2:
time: 84.3 us; the launch traced here: 84.2 us
  Pallas kernels  81.1 us (96%)
  local copies, waits for them, and re-layouts  3.05 us (4%)
    pallas_call x1, Pallas kernels, body(): pl.pallas_call(solve_kernel, out_shape=jax.ShapeDtypeStruct((ROWS, W), f3...  81.1 us
    unnamed x1, local copies, waits for them, and re-layouts  3.05 us

profile of v2, /device:TPU:1, one launch (start us, length us, event | category | flops | bytes accessed | tf_op | source)
XLA Modules:
  0.0 84.2 jit_solution(13736660281695246903)
XLA Ops:
  0.0 81.1 %solve.1 = f32[4096,128]{1,0:T(8,128)} custom-call(f32[4096,128]{1,0:T(8,128)} %l4.1, f32[4096,128]{1,0:T(8,128)} %l3.1, f32[4096,128]{1,0:T(8,128)} %l2.1, f32[4096,128]{1,0:T(8,128)} %l1.1, f32[4096,128]{1,0:T(8,128)} %x_in.1, f32[4096,128]{1,0:T(8,128)} %r4.1, f32[4096,128]{1,0:T(8,128)} %r3.1, f32[4096,128]{1,0:T(8,128)} %r2.1, f32[4096,128]{1,0:T(8,128)} %r1.1), custom_call_target="tpu_custom_call" | custom-call | tf_op jit(solution)/shard_map/solve/pallas_call | solution.py:324
  81.2 3.0 %copy.11 = f32[4096,128]{1,0:T(8,128)} copy(f32[4096,128]{1,0:T(8,128)} %solve.1) | data formatting | bytes 4194304

commit v3 on v0

v3 whole, which is shorter than its diff:
```python
import functools

import jax
import jax.numpy as jnp
from jax import lax
from jax.experimental import pallas as pl
from jax.experimental.pallas import tpu as pltpu
from jax.sharding import PartitionSpec as P

W = 128
HALF = 64
ROWS = 4096
CHUNK = 1024
CHUNKS = ROWS // CHUNK
HIGH = lax.Precision.HIGH
HIGHEST = lax.Precision.HIGHEST
MESH = pl.DeviceIdType.MESH


def dot(a, b, precision=HIGHEST):
    return jnp.dot(a, b, precision=precision, preferred_element_type=jnp.float32)


def split(v):
    high = v.astype(jnp.bfloat16)
    low = (v - high.astype(jnp.float32)).astype(jnp.bfloat16)
    return high, low


def inverse(matrix, between=None):
    lane = lax.broadcasted_iota(jnp.int32, (8, W), 1)
    sub = lax.broadcasted_iota(jnp.int32, (8, W), 0)
    lane_half = lax.broadcasted_iota(jnp.int32, (HALF, W), 1)
    row_whole = lax.broadcasted_iota(jnp.int32, (W, W), 0)

    def column(tile, index):
        return jnp.take_along_axis(tile, jnp.full((8, W), index, jnp.int32), axis=1, mode="promise_in_bounds")

    def spread(tile, i):
        return jnp.broadcast_to(tile[i : i + 1], (8, W))

    def block_step(block, halves):
        start = block * HALF
        panel, rest = halves
        tiles = [panel[8 * i : 8 * i + 8] for i in range(8)]
        for step in range(8):
            begin = start + 8 * step
            inside = (lane >= begin) & (lane < begin + 8)
            cols = [column(tiles[step], begin + i) for i in range(8)]
            pivot = jnp.where(inside, jnp.where(lane == begin + sub, 1.0, 0.0), tiles[step])
            for i in range(0, 8, 2):
                left, right = cols[i], cols[i + 1]
                a, b, c, d = spread(left, i), spread(right, i), spread(left, i + 1), spread(right, i + 1)
                inv = 1.0 / (a * d - b * c)
                at_one, at_two = sub == i, sub == i + 1

                def sweep(tile):
                    one, two = spread(tile, i), spread(tile, i + 1)
                    first = (d * one - b * two) * inv
                    second = (a * two - c * one) * inv
                    other = tile - (left * first + right * second)
                    return jnp.where(at_one, first, jnp.where(at_two, second, other))

                for j in range(i + 2, 8):
                    cols[j] = sweep(cols[j])
                pivot = sweep(pivot)
            rows = [jnp.broadcast_to(pivot[i : i + 1], (8, W)) for i in range(8)]
            for t in range(8):
                if t == step:
                    continue
                terms = [column(tiles[t], begin + i) * rows[i] for i in range(8)]
                while len(terms) > 1:
                    terms = [terms[k] + terms[k + 1] for k in range(0, len(terms), 2)]
                tiles[t] = jnp.where(inside, 0.0, tiles[t]) - terms[0]
            tiles[step] = pivot
        panel = jnp.concatenate(tiles, axis=0)
        tall = jnp.where(
            (row_whole >= start) & (row_whole < start + HALF), jnp.concatenate([panel, panel], axis=0), 0.0
        )
        inside = (lane_half >= start) & (lane_half < start + HALF)
        return jnp.where(inside, 0.0, rest) - dot(rest, tall), panel

    halves = (matrix[:HALF], matrix[HALF:])
    if between is None:
        halves = lax.fori_loop(0, 2, block_step, halves)
    else:
        halves = lax.fori_loop(0, 1, block_step, halves)
        between()
        halves = lax.fori_loop(1, 2, block_step, halves)
    return jnp.concatenate(halves, axis=0)


def solve_kernel(
    l4, l3, l2, l1, x_in, r4, r3, r2, r1, out, a_buf, r_buf, r_high, r_low, acc, h, rx0, rx1, half, rx2,
    own, rest, gat, gatx, us, inv_buf, load_sems, out_sems, sems,
):
    z = lax.axis_index("outer")
    inner = lax.axis_index("inner")
    x = inner // 8
    y = lax.rem(inner, 8) // 2
    core = lax.rem(inner, 2)
    mine = core * 4 + y

    def load(refs, buffer, offset, k):
        chunks = []
        for c in range(CHUNKS):
            rows = pl.ds(c * CHUNK, CHUNK)
            chunks.append([
                pltpu.make_async_copy(ref.at[rows, :], buffer.at[offset + i, rows, :], load_sems.at[k + i, c])
                for i, ref in enumerate(refs)
            ])
        return chunks

    loads = [r + a for r, a in zip(load((r4, r3, r2, r1), r_buf, 0, 0), load((l4, l3), a_buf, 0, 4))]
    late_loads = load((l2, l1, x_in), a_buf, 2, 6)
    for chunk in loads + late_loads:
        for copy in chunk:
            copy.start()

    def device(z_to, x_to, dy, dc):
        y_to = lax.rem(y + dy, 4)
        c_to = lax.rem(core + dc, 2)
        return (z_to, x_to * 8 + y_to * 2 + c_to)

    partners = (
        (z, x + 1 - 2 * lax.rem(x, 2)),
        (z, lax.rem(x + 2, 4)),
        (z + 1 - 2 * lax.rem(z, 2), x),
        (lax.rem(z + 2, 4), x),
    )
    around = [(dy, dc) for dy in (2, 1, 3, 0) for dc in (1, 0)]
    near = [(z, x, dy, dc) for dy, dc in around[:7]]
    far = [[(zp, xp, dy, dc) for dy, dc in around] for zp, xp in partners]
    peers = far[3] + far[1] + far[2] + far[0] + near
    barrier = pltpu.get_barrier_semaphore()
    for peer in peers:
        pl.semaphore_signal(barrier, inc=1, device_id=device(*peer), device_id_type=MESH)

    count = [0]
    started = []

    def send(src, dst, to):
        k = count[0]
        count[0] += 1
        copy = pltpu.make_async_remote_copy(
            src_ref=src, dst_ref=dst, send_sem=sems.at[0, k], recv_sem=sems.at[1, k],
            device_id=device(*to), device_id_type=MESH,
        )
        copy.start()
        started.append(copy)
        return copy

    def receive(copies):
        for copy in copies:
            copy.wait_recv()

    one = functools.partial(jnp.dot, preferred_element_type=jnp.float32)

    def product(blocks, rows, high, low):
        parts = [split(a_buf[i, rows, :].T) for i in blocks]
        a_high = jnp.concatenate([part[0] for part in parts], axis=0)
        a_low = jnp.concatenate([part[1] for part in parts], axis=0)
        return one(a_high, high) + one(a_low, high) + one(a_high, low)

    total = None
    for c in range(CHUNKS):
        rows = pl.ds(c * CHUNK, CHUNK)
        for copy in loads[c]:
            copy.wait()
        high, low = split(jnp.concatenate([r_buf[i, rows, :] for i in range(4)], axis=1))
        r_high[rows, :] = high
        r_low[rows, :] = low
        total = product((0, 1), rows, high, low)
        if c > 0:
            total = acc[0 : 2 * W, :] + total
        if c < CHUNKS - 1:
            acc[0 : 2 * W, :] = total
    h[0][...] = total[:W].reshape(2, 4, 16, 512)
    h[1][...] = total[W:].reshape(2, 4, 16, 512)
    pl.semaphore_wait(barrier, len(peers))

    def late_product(c):
        rows = pl.ds(c * CHUNK, CHUNK)
        for copy in late_loads[c]:
            copy.wait()
        total = product((2, 3, 4), rows, r_high[rows, :], r_low[rows, :])
        if c > 0:
            total = acc[...] + total
        if c < CHUNKS - 1:
            acc[...] = total
        else:
            h[2][...] = total[:W].reshape(2, 4, 16, 512)
            h[3][:, :, 0:16, :] = total[W : 2 * W].reshape(2, 4, 16, 512)
            h[3][:, :, 16:32, :] = total[2 * W :].reshape(2, 4, 16, 512)

    mine_rows = pl.ds(pl.multiple_of(mine * 16, 16), 16)
    pivots = [[] for _ in range(4)]
    others = [[] for _ in range(4)]
    nexts = [[] for _ in range(4)]
    rests = [[] for _ in range(4)]

    def send_pivot_rows(level):
        mat, gather = own[level], gat[level]
        for side, targets in ((1, far[level]), (0, near)):
            for to in targets:
                pivots[level].append(send(mat.at[0:16, 0:W], gather.at[side, mine_rows, 0:W], to))
        gather[0, mine_rows, 0:W] = mat[0:16, 0:W]

    def send_side_rows(level):
        for side, targets in ((1, far[level]), (0, near)):
            for to in targets:
                if level < 2 and to[3] == 1:
                    continue
                if level < 3:
                    copy = send(own[level].at[0:16, W:], gat[level].at[side, mine_rows, W:], to)
                else:
                    copy = send(own[3].at[16:32, :], gatx.at[side, mine_rows, :], to)
                others[level].append(copy)
        if level == 3:
            gatx[0, mine_rows, :] = own[3][16:32, :]
        else:
            gat[level][0, mine_rows, W:] = own[level][0:16, W:]

    first = [None] * 4
    second = [None] * 4

    def send_core(piece):
        low = W if piece == 0 else 0
        first[piece] = send(h[piece].at[1 - core, :, :, low:], rx1[piece], (z, x, 0, 1))

    def sum_cores(piece):
        receive([first[piece]])
        low = W if piece == 0 else 0
        half[piece][...] = h[piece][core, :, :, low:] + rx1[piece][...]

    def send_chips(piece):
        second[piece] = [
            send(half[piece].at[lax.rem(y + dy, 4)], rx2[piece].at[dy - 1], (z, x, dy, 0)) for dy in (2, 1, 3)
        ]

    def sum_chips(piece, rows):
        receive(second[piece])
        low = W if piece == 0 else 0
        own[0][rows, low:] = half[piece][y] + rx2[piece][0] + rx2[piece][1] + rx2[piece][2]

    direct = []
    for k, (_, _, dy, dc) in enumerate(near):
        piece = h[0].at[lax.rem(core + dc, 2), lax.rem(y + dy, 4), :, 0:W]
        direct.append(send(piece, rx0.at[k], (z, x, dy, dc)))
    send_core(0)
    send_core(1)
    late_product(0)
    sum_cores(0)
    send_chips(0)
    late_product(1)
    receive(direct)
    couplings = h[0][core, y, :, 0:W]
    for k in range(7):
        couplings = couplings + rx0[k]
    own[0][0:16, 0:W] = couplings
    send_pivot_rows(0)
    sum_cores(1)
    send_chips(1)
    late_product(2)
    sum_chips(0, slice(0, 16))
    send_side_rows(0)
    late_product(3)
    send_core(2)
    send_core(3)
    sum_chips(1, slice(16, 32))
    nexts[0].append(send(own[0].at[16:32, :], rest[0].at[0:16, :], partners[0] + (0, 0)))
    for piece in (2, 3):
        sum_cores(piece)
        send_chips(piece)

    eye = jnp.where(
        lax.broadcasted_iota(jnp.int32, (W, W), 0) == lax.broadcasted_iota(jnp.int32, (W, W), 1), 1.0, 0.0
    )
    spread = [[] for _ in range(3)]

    def apply(targets, sources, weights, between):
        w_high, w_low = split(weights.T)
        size = 512
        for c in range(ROWS // size):
            if c == 2:
                between()
            rows = pl.ds(c * size, size)
            wide = [a_buf[i, rows, :] for i in sources]
            high, low = split(wide[0] if len(wide) == 1 else jnp.concatenate(wide, axis=1))
            change = one(high, w_high) + one(low, w_high) + one(high, w_low)
            for k, target in enumerate(targets):
                a_buf[target, rows, :] = a_buf[target, rows, :] - change[:, W * k : W * k + W]

    def blocks(level, b):
        return us[level][:, 16 * b : 16 * b + 16, :].reshape(W, W)

    core_rows = pl.ds(pl.multiple_of(core * 64, 64), 64)
    forward = [[], []]
    coef_forward = [[], []]

    def forward_side_rows(level):
        receive(others[level])
        both = gat[level].at[:, core_rows, W:]
        forward[level].append(send(both, both, (z, x, 0, 1)))

    def forward_coefficients(level):
        receive(spread[level])
        half_of = us[level].at[pl.ds(core * 4, 4)]
        coef_forward[level].append(send(half_of, half_of, (z, x, 0, 1)))

    def send_partner(level, low, top, copies):
        target = rest[level].at[low - 16 : top - 16, :]
        copies[level].append(send(own[level].at[low:top, :], target, partners[level] + (0, 0)))

    def send_coefficients(level):
        for to in near:
            if level < 2 and to[3] == 1:
                continue
            spread[level].append(send(us[level].at[mine], us[level].at[mine], to))

    def advance(level, low, top, copies):
        receive(copies[level])
        gather, inv = gat[level], inv_buf[...]
        p_own, p_sib = gather[0, :, 0:W], gather[1, :, 0:W]
        w_own = own[level][low:top, 0:W]
        w_sib = rest[level][low - 16 : top - 16, 0:W]
        u_own = dot(w_sib - dot(w_own, p_sib), inv)
        u_sib = w_own - dot(u_own, p_own)
        us[level][mine, low - 16 : top - 16, :] = u_own
        own[level + 1][low - 16 : top - 16, :] = (
            own[level][low:top, W:]
            + rest[level][low - 16 : top - 16, W:]
            - dot(u_own, gather[0, :, W:])
            - dot(u_sib, gather[1, :, W:])
        )

    def solve_pivots(level, between=None):
        receive(pivots[level])
        return inverse(eye - dot(gat[level][0, :, 0:W], gat[level][1, :, 0:W]), between)

    mids = [[] for _ in range(4)]

    inv_buf[...] = solve_pivots(0, functools.partial(forward_side_rows, 0))
    receive(forward[0])
    advance(0, 16, 32, nexts)
    send_pivot_rows(1)
    sum_chips(2, slice(32, 48))
    send_partner(0, 32, 48, mids)
    send_side_rows(1)
    sum_chips(3, slice(48, 80))
    send_partner(0, 48, 80, rests)
    advance(0, 32, 48, mids)
    send_partner(1, 16, 32, nexts)

    def late_rows():
        forward_side_rows(1)
        advance(0, 48, 80, rests)
        send_partner(1, 32, 64, rests)
        send_coefficients(0)

    inv = solve_pivots(1, late_rows)
    inv_buf[...] = inv
    receive(forward[1])
    advance(1, 16, 32, nexts)
    send_pivot_rows(2)
    advance(1, 32, 64, rests)

    send_partner(2, 16, 32, nexts)
    send_side_rows(2)
    send_partner(2, 32, 48, rests)
    send_coefficients(1)
    forward_coefficients(0)
    inv_buf[...] = solve_pivots(2)
    receive(others[2])
    forward_coefficients(1)
    advance(2, 16, 32, nexts)
    send_pivot_rows(3)
    advance(2, 32, 48, rests)

    receive(coef_forward[0] + coef_forward[1])
    def last_sends():
        send_side_rows(3)
        send_coefficients(2)

    u3 = jnp.concatenate([blocks(1, b) for b in range(3)], axis=0)
    u4 = jnp.concatenate([blocks(0, b) for b in range(1, 4)], axis=0) - dot(u3, blocks(0, 0))
    apply((2, 3, 4), (0, 1), jnp.concatenate([u4, u3], axis=1), last_sends)
    for copy in started[:-22]:
        copy.wait_send()
    del started[:-22]
    inv = solve_pivots(3)
    receive(others[3])
    y_one = dot(gatx[1] - dot(gatx[0], gat[3][1]), inv)

    receive(spread[2])
    y_two = blocks(2, 1) - dot(y_one, blocks(2, 0))
    w_high, w_low = split(jnp.concatenate([y_two.T, y_one.T], axis=0))
    w_both = jnp.concatenate([w_high, w_low], axis=1)
    stores = []
    size = ROWS // 8
    for c in range(8):
        rows = pl.ds(c * size, size)
        high, low = split(jnp.concatenate([a_buf[2, rows, :], a_buf[3, rows, :]], axis=1))
        both = one(high, w_both)
        a_buf[4, rows, :] = a_buf[4, rows, :] - (both[:, :W] + both[:, W:] + one(low, w_high))
        stores.append(pltpu.make_async_copy(a_buf.at[4, rows, :], out.at[rows, :], out_sems.at[c]))
        stores[-1].start()
    for copy in stores:
        copy.wait()
    for copy in started:
        copy.wait_send()


def body(l4, l3, l2, l1, r4, r3, r2, r1, x):
    f32 = jnp.float32
    hbm = pl.BlockSpec(memory_space=pl.ANY)
    pieces, widths = (16, 16, 16, 32), (384, 512, 512, 512)
    n_copies = 7 + 4 + 12 + 4 * 15 + 2 * 8 + 2 * 15 + 7 + 2 * 4 + 7
    return pl.pallas_call(
        solve_kernel,
        out_shape=jax.ShapeDtypeStruct((ROWS, W), f32),
        in_specs=[hbm] * 9,
        out_specs=hbm,
        scratch_shapes=[
            pltpu.VMEM((5, ROWS, W), f32),
            pltpu.VMEM((4, ROWS, W), f32),
            pltpu.VMEM((ROWS, 512), jnp.bfloat16),
            pltpu.VMEM((ROWS, 512), jnp.bfloat16),
            pltpu.VMEM((384, 512), f32),
            [pltpu.VMEM((2, 4, n, 512), f32) for n in pieces],
            pltpu.VMEM((7, 16, W), f32),
            [pltpu.VMEM((4, n, lanes), f32) for n, lanes in zip(pieces, widths)],
            [pltpu.VMEM((4, n, lanes), f32) for n, lanes in zip(pieces, widths)],
            [pltpu.VMEM((3, n, lanes), f32) for n, lanes in zip(pieces, widths)],
            [pltpu.VMEM((16 * (5 - k), W * (4 - k)), f32) for k in range(4)],
            [pltpu.VMEM((16 * (4 - k), W * (4 - k)), f32) for k in range(3)],
            [pltpu.VMEM((2, W, W * (4 - k)), f32) for k in range(4)],
            pltpu.VMEM((2, W, W), f32),
            [pltpu.VMEM((8, 16 * (4 - k), W), f32) for k in range(3)],
            pltpu.VMEM((W, W), f32),
            pltpu.SemaphoreType.DMA((9, CHUNKS)),
            pltpu.SemaphoreType.DMA((8,)),
            pltpu.SemaphoreType.DMA((2, n_copies)),
        ],
        compiler_params=pltpu.CompilerParams(
            collective_id=0, has_side_effects=True, vmem_limit_bytes=60 * 1024 * 1024
        ),
        name="solve",
    )(l4, l3, l2, l1, x, r4, r3, r2, r1)


def solution(mesh):
    spec = P(("outer", "inner"), None)
    return jax.shard_map(body, mesh=mesh, in_specs=(spec,) * 9, out_specs=spec, check_vma=False)
```

time: 1070 us -> 62 us (0.06); the launches traced: 1050 us -> 61.8 us
  local copies, waits for them, and re-layouts: 453 us -> 3.05 us
  other arithmetic: 385 us -> 0 us
  waiting for transfers between devices: 76.8 us -> 0 us
  matrix products: 67.5 us -> 0 us
  Pallas kernels: 0 us -> 58.8 us
  starting transfers between devices: 47.9 us -> 0 us
  loops' own time: 23.9 us -> 0 us
    dynamic_slice x1024 -> x0, local copies, waits for them, and re-layouts: 405 us -> none  [the longest x512 315 us: pivot_step(): pivot_value = lax.dynamic_slice_in_dim(pivot_row, pivot_index, 1, 1)]
    div x512 -> x0, other arithmetic: 328 us -> none  [pivot_step(): pivot_row = pivot_row / pivot_value]
    ppermute x22 -> x0, waiting for transfers between devices: 76.8 us -> none  [partner(): return lax.ppermute(value, axis, pairs)]
    dot_general x16 -> x0, matrix products: 67.5 us -> none  [the longest x4 33.5 us: body(): jnp.dot(basis, coefficients, precision=highest, preferred_element_type=jn...]
    pallas_call x0 -> x1, Pallas kernels: none -> 58.8 us  [body(): pl.pallas_call(solve_kernel, out_shape=jax.ShapeDtypeStruct((ROWS, W), f3...]
    sub x512 -> x0, other arithmetic: 56.8 us -> none  [pivot_step(): matrix = matrix - column * pivot_row]
    ppermute x22 -> x0, starting transfers between devices: 47.9 us -> none  [partner(): return lax.ppermute(value, axis, pairs)]
    dynamic_update_slice x512 -> x0, local copies, waits for them, and re-layouts: 29.9 us -> none  [pivot_step(): return lax.dynamic_update_slice_in_dim(matrix, pivot_row, pivot_index, 0)]
  transfers between devices with their start and end apart: 22 -> 0, of which waited for: 21 -> 0; matrix products, arithmetic and copies ran while one was open for 1% -> 0% of each run, Pallas kernels for 0% -> 0%
where the time goes in v3:
time: 62 us; the launch traced here: 61.8 us
  Pallas kernels  58.8 us (95%)
  local copies, waits for them, and re-layouts  3.05 us (5%)
    pallas_call x1, Pallas kernels, body(): pl.pallas_call(solve_kernel, out_shape=jax.ShapeDtypeStruct((ROWS, W), f3...  58.8 us
    unnamed x1, local copies, waits for them, and re-layouts  3.05 us

profile of v3, /device:TPU:1, one launch (start us, length us, event | category | flops | bytes accessed | tf_op | source)
XLA Modules:
  0.0 61.8 jit_solution(6229539845141983227)
XLA Ops:
  0.0 58.8 %solve.1 = f32[4096,128]{1,0:T(8,128)} custom-call(f32[4096,128]{1,0:T(8,128)} %l4.1, f32[4096,128]{1,0:T(8,128)} %l3.1, f32[4096,128]{1,0:T(8,128)} %l2.1, f32[4096,128]{1,0:T(8,128)} %l1.1, f32[4096,128]{1,0:T(8,128)} %x_in.1, f32[4096,128]{1,0:T(8,128)} %r4.1, f32[4096,128]{1,0:T(8,128)} %r3.1, f32[4096,128]{1,0:T(8,128)} %r2.1, f32[4096,128]{1,0:T(8,128)} %r1.1), custom_call_target="tpu_custom_call" | custom-call | tf_op jit(solution)/shard_map/solve/pallas_call | solution.py:419
  58.8 3.0 %copy.11 = f32[4096,128]{1,0:T(8,128)} copy(f32[4096,128]{1,0:T(8,128)} %solve.1) | data formatting | bytes 4194304

commit v4 on v3

--- a/solution.py
+++ b/solution.py
@@ -92,7 +92,7 @@
 
 def solve_kernel(
     l4, l3, l2, l1, x_in, r4, r3, r2, r1, out, a_buf, r_buf, r_high, r_low, acc, h, rx0, rx1, half, rx2,
-    own, rest, gat, gatx, us, inv_buf, load_sems, out_sems, sems,
+    own, rest, gat, gatx, us, inv_buf, load_sems, sems,
 ):
     z = lax.axis_index("outer")
     inner = lax.axis_index("inner")
@@ -100,22 +100,6 @@
     y = lax.rem(inner, 8) // 2
     core = lax.rem(inner, 2)
     mine = core * 4 + y
-
-    def load(refs, buffer, offset, k):
-        chunks = []
-        for c in range(CHUNKS):
-            rows = pl.ds(c * CHUNK, CHUNK)
-            chunks.append([
-                pltpu.make_async_copy(ref.at[rows, :], buffer.at[offset + i, rows, :], load_sems.at[k + i, c])
-                for i, ref in enumerate(refs)
-            ])
-        return chunks
-
-    loads = [r + a for r, a in zip(load((r4, r3, r2, r1), r_buf, 0, 0), load((l4, l3), a_buf, 0, 4))]
-    late_loads = load((l2, l1, x_in), a_buf, 2, 6)
-    for chunk in loads + late_loads:
-        for copy in chunk:
-            copy.start()
 
     def device(z_to, x_to, dy, dc):
         y_to = lax.rem(y + dy, 4)
@@ -135,6 +119,22 @@
     barrier = pltpu.get_barrier_semaphore()
     for peer in peers:
         pl.semaphore_signal(barrier, inc=1, device_id=device(*peer), device_id_type=MESH)
+
+    def load(refs, buffer, offset, k):
+        chunks = []
+        for c in range(CHUNKS):
+            rows = pl.ds(c * CHUNK, CHUNK)
+            chunks.append([
+                pltpu.make_async_copy(ref.at[rows, :], buffer.at[offset + i, rows, :], load_sems.at[k + i, c])
+                for i, ref in enumerate(refs)
+            ])
+        return chunks
+
+    loads = [r + a for r, a in zip(load((r4, r3, r2, r1), r_buf, 0, 0), load((l4, l3), a_buf, 0, 4))]
+    late_loads = load((l2, l1, x_in), a_buf, 2, 6)
+    for chunk in loads + late_loads:
+        for copy in chunk:
+            copy.start()
 
     count = [0]
     started = []
@@ -250,8 +250,9 @@
     send_core(0)
     send_core(1)
     late_product(0)
-    sum_cores(0)
-    send_chips(0)
+    for piece in (0, 1):
+        sum_cores(piece)
+        send_chips(piece)
     late_product(1)
     receive(direct)
     couplings = h[0][core, y, :, 0:W]
@@ -259,8 +260,6 @@
         couplings = couplings + rx0[k]
     own[0][0:16, 0:W] = couplings
     send_pivot_rows(0)
-    sum_cores(1)
-    send_chips(1)
     late_product(2)
     sum_chips(0, slice(0, 16))
     send_side_rows(0)
@@ -282,7 +281,7 @@
         w_high, w_low = split(weights.T)
         size = 512
         for c in range(ROWS // size):
-            if c == 2:
+            if c == 5:
                 between()
             rows = pl.ds(c * size, size)
             wide = [a_buf[i, rows, :] for i in sources]
@@ -324,14 +323,14 @@
         p_own, p_sib = gather[0, :, 0:W], gather[1, :, 0:W]
         w_own = own[level][low:top, 0:W]
         w_sib = rest[level][low - 16 : top - 16, 0:W]
-        u_own = dot(w_sib - dot(w_own, p_sib), inv)
-        u_sib = w_own - dot(u_own, p_own)
+        u_own = dot(w_sib - dot(w_own, p_sib, HIGH), inv, HIGH)
+        u_sib = w_own - dot(u_own, p_own, HIGH)
         us[level][mine, low - 16 : top - 16, :] = u_own
         own[level + 1][low - 16 : top - 16, :] = (
             own[level][low:top, W:]
             + rest[level][low - 16 : top - 16, W:]
-            - dot(u_own, gather[0, :, W:])
-            - dot(u_sib, gather[1, :, W:])
+            - dot(u_own, gather[0, :, W:], HIGH)
+            - dot(u_sib, gather[1, :, W:], HIGH)
         )
 
     def solve_pivots(level, between=None):
@@ -396,17 +395,12 @@
     y_two = blocks(2, 1) - dot(y_one, blocks(2, 0))
     w_high, w_low = split(jnp.concatenate([y_two.T, y_one.T], axis=0))
     w_both = jnp.concatenate([w_high, w_low], axis=1)
-    stores = []
     size = ROWS // 8
     for c in range(8):
         rows = pl.ds(c * size, size)
         high, low = split(jnp.concatenate([a_buf[2, rows, :], a_buf[3, rows, :]], axis=1))
         both = one(high, w_both)
-        a_buf[4, rows, :] = a_buf[4, rows, :] - (both[:, :W] + both[:, W:] + one(low, w_high))
-        stores.append(pltpu.make_async_copy(a_buf.at[4, rows, :], out.at[rows, :], out_sems.at[c]))
-        stores[-1].start()
-    for copy in stores:
-        copy.wait()
+        out[rows, :] = a_buf[4, rows, :] - (both[:, :W] + both[:, W:] + one(low, w_high))
     for copy in started:
         copy.wait_send()
 
@@ -420,7 +414,7 @@
         solve_kernel,
         out_shape=jax.ShapeDtypeStruct((ROWS, W), f32),
         in_specs=[hbm] * 9,
-        out_specs=hbm,
+        out_specs=pl.BlockSpec(memory_space=pltpu.VMEM),
         scratch_shapes=[
             pltpu.VMEM((5, ROWS, W), f32),
             pltpu.VMEM((4, ROWS, W), f32),
@@ -439,11 +433,10 @@
             [pltpu.VMEM((8, 16 * (4 - k), W), f32) for k in range(3)],
             pltpu.VMEM((W, W), f32),
             pltpu.SemaphoreType.DMA((9, CHUNKS)),
-            pltpu.SemaphoreType.DMA((8,)),
             pltpu.SemaphoreType.DMA((2, n_copies)),
         ],
         compiler_params=pltpu.CompilerParams(
-            collective_id=0, has_side_effects=True, vmem_limit_bytes=60 * 1024 * 1024
+            collective_id=0, has_side_effects=True, vmem_limit_bytes=50 * 1024 * 1024
         ),
         name="solve",
     )(l4, l3, l2, l1, x, r4, r3, r2, r1)

time: 62 us -> 58.6 us (0.945)
  local copies, waits for them, and re-layouts: 3.05 us -> 1.32 us
  Pallas kernels: 58.8 us -> 57.1 us
    unnamed x1, local copies, waits for them, and re-layouts: 3.05 us -> 1.32 us
    pallas_call x1, Pallas kernels: 58.8 us -> 57.1 us  [body(): pl.pallas_call(solve_kernel, out_shape=jax.ShapeDtypeStruct((ROWS, W), f3...]
where the time goes in v4:
time: 58.6 us; the launch traced here: 58.5 us
  Pallas kernels  57.1 us (97%)
  local copies, waits for them, and re-layouts  1.32 us (2%)
    pallas_call x1, Pallas kernels, body(): pl.pallas_call(solve_kernel, out_shape=jax.ShapeDtypeStruct((ROWS, W), f3...  57.1 us
    unnamed x1, local copies, waits for them, and re-layouts  1.32 us

profile of v4, /device:TPU:1, one launch (start us, length us, event | category | flops | bytes accessed | tf_op | source)
XLA Modules:
  0.0 58.5 jit_solution(17254422573090496448)
XLA Ops:
  0.0 57.1 %solve.1 = f32[4096,128]{1,0:T(8,128)S(1)} custom-call(f32[4096,128]{1,0:T(8,128)} %l4.1, f32[4096,128]{1,0:T(8,128)} %l3.1, f32[4096,128]{1,0:T(8,128)} %l2.1, f32[4096,128]{1,0:T(8,128)} %l1.1, f32[4096,128]{1,0:T(8,128)} %x_in.1, f32[4096,128]{1,0:T(8,128)} %r4.1, f32[4096,128]{1,0:T(8,128)} %r3.1, f32[4096,128]{1,0:T(8,128)} %r2.1, f32[4096,128]{1,0:T(8,128)} %r1.1), custom_call_target="tpu_custom_call" | custom-call | tf_op jit(solution)/shard_map/solve/pallas_call | solution.py:413
  57.1 1.3 %copy.11 = f32[4096,128]{1,0:T(8,128)} copy(f32[4096,128]{1,0:T(8,128)S(1)} %solve.1) | data formatting | bytes 4194304

commit v5 on v4

--- a/solution.py
+++ b/solution.py
@@ -81,12 +81,10 @@
         return jnp.where(inside, 0.0, rest) - dot(rest, tall), panel
 
     halves = (matrix[:HALF], matrix[HALF:])
-    if between is None:
-        halves = lax.fori_loop(0, 2, block_step, halves)
-    else:
-        halves = lax.fori_loop(0, 1, block_step, halves)
+    halves = block_step(0, halves)
+    if between is not None:
         between()
-        halves = lax.fori_loop(1, 2, block_step, halves)
+    halves = block_step(1, halves)
     return jnp.concatenate(halves, axis=0)
 
 
@@ -281,7 +279,7 @@
         w_high, w_low = split(weights.T)
         size = 512
         for c in range(ROWS // size):
-            if c == 5:
+            if c == 2:
                 between()
             rows = pl.ds(c * size, size)
             wide = [a_buf[i, rows, :] for i in sources]
@@ -295,12 +293,15 @@
 
     core_rows = pl.ds(pl.multiple_of(core * 64, 64), 64)
     forward = [[], []]
+    forward_late = [[], []]
     coef_forward = [[], []]
 
     def forward_side_rows(level):
         receive(others[level])
-        both = gat[level].at[:, core_rows, W:]
+        both = gat[level].at[:, core_rows, W : 2 * W]
         forward[level].append(send(both, both, (z, x, 0, 1)))
+        both = gat[level].at[:, core_rows, 2 * W :]
+        forward_late[level].append(send(both, both, (z, x, 0, 1)))
 
     def forward_coefficients(level):
         receive(spread[level])
@@ -333,6 +334,29 @@
             - dot(u_sib, gather[1, :, W:], HIGH)
         )
 
+    def advance_pivots(level):
+        receive(nexts[level])
+        gather, inv = gat[level], inv_buf[...]
+        p_own, p_sib = gather[0, :, 0:W], gather[1, :, 0:W]
+        w_own = own[level][16:32, 0:W]
+        u_own = dot(rest[level][0:16, 0:W] - dot(w_own, p_sib, HIGH), inv, HIGH)
+        u_sib = w_own - dot(u_own, p_own, HIGH)
+        us[level][mine, 0:16, :] = u_own
+
+        def pass_on(low, top):
+            own[level + 1][0:16, low - W : top - W] = (
+                own[level][16:32, low:top]
+                + rest[level][0:16, low:top]
+                - dot(u_own, gather[0, :, low:top], HIGH)
+                - dot(u_sib, gather[1, :, low:top], HIGH)
+            )
+
+        pass_on(W, 2 * W)
+        send_pivot_rows(level + 1)
+        if level < 2:
+            receive(forward_late[level])
+            pass_on(2 * W, (4 - level) * W)
+
     def solve_pivots(level, between=None):
         receive(pivots[level])
         return inverse(eye - dot(gat[level][0, :, 0:W], gat[level][1, :, 0:W]), between)
@@ -341,8 +365,7 @@
 
     inv_buf[...] = solve_pivots(0, functools.partial(forward_side_rows, 0))
     receive(forward[0])
-    advance(0, 16, 32, nexts)
-    send_pivot_rows(1)
+    advance_pivots(0)
     sum_chips(2, slice(32, 48))
     send_partner(0, 32, 48, mids)
     send_side_rows(1)
@@ -355,25 +378,23 @@
         forward_side_rows(1)
         advance(0, 48, 80, rests)
         send_partner(1, 32, 64, rests)
-        send_coefficients(0)
 
     inv = solve_pivots(1, late_rows)
     inv_buf[...] = inv
     receive(forward[1])
-    advance(1, 16, 32, nexts)
-    send_pivot_rows(2)
+    advance_pivots(1)
     advance(1, 32, 64, rests)
 
+    send_side_rows(2)
     send_partner(2, 16, 32, nexts)
-    send_side_rows(2)
     send_partner(2, 32, 48, rests)
+    send_coefficients(0)
     send_coefficients(1)
-    forward_coefficients(0)
     inv_buf[...] = solve_pivots(2)
     receive(others[2])
+    forward_coefficients(0)
     forward_coefficients(1)
-    advance(2, 16, 32, nexts)
-    send_pivot_rows(3)
+    advance_pivots(2)
     advance(2, 32, 48, rests)
 
     receive(coef_forward[0] + coef_forward[1])
@@ -409,7 +430,7 @@
     f32 = jnp.float32
     hbm = pl.BlockSpec(memory_space=pl.ANY)
     pieces, widths = (16, 16, 16, 32), (384, 512, 512, 512)
-    n_copies = 7 + 4 + 12 + 4 * 15 + 2 * 8 + 2 * 15 + 7 + 2 * 4 + 7
+    n_copies = 7 + 4 + 12 + 4 * 15 + 2 * 9 + 2 * 15 + 7 + 2 * 4 + 7
     return pl.pallas_call(
         solve_kernel,
         out_shape=jax.ShapeDtypeStruct((ROWS, W), f32),

time: 58.6 us -> 58.1 us (level)
  no operation moved by 1% of the time
where the time goes in v5:
time: 58.1 us; the launch traced here: 58 us
  Pallas kernels  56.7 us (98%)
  local copies, waits for them, and re-layouts  1.32 us (2%)
    pallas_call x1, Pallas kernels, body(): pl.pallas_call(solve_kernel, out_shape=jax.ShapeDtypeStruct((ROWS, W), f3...  56.7 us
    unnamed x1, local copies, waits for them, and re-layouts  1.32 us

profile of v5, /device:TPU:1, one launch (start us, length us, event | category | flops | bytes accessed | tf_op | source)
XLA Modules:
  0.0 58.0 jit_solution(320784918196887837)
XLA Ops:
  0.0 56.7 %solve.1 = f32[4096,128]{1,0:T(8,128)S(1)} custom-call(f32[4096,128]{1,0:T(8,128)} %l4.1, f32[4096,128]{1,0:T(8,128)} %l3.1, f32[4096,128]{1,0:T(8,128)} %l2.1, f32[4096,128]{1,0:T(8,128)} %l1.1, f32[4096,128]{1,0:T(8,128)} %x_in.1, f32[4096,128]{1,0:T(8,128)} %r4.1, f32[4096,128]{1,0:T(8,128)} %r3.1, f32[4096,128]{1,0:T(8,128)} %r2.1, f32[4096,128]{1,0:T(8,128)} %r1.1), custom_call_target="tpu_custom_call" | custom-call | tf_op jit(solution)/shard_map/solve/pallas_call | solution.py:434
  56.7 1.3 %copy.11 = f32[4096,128]{1,0:T(8,128)} copy(f32[4096,128]{1,0:T(8,128)S(1)} %solve.1) | data formatting | bytes 4194304

commit v6 on v5

--- a/solution.py
+++ b/solution.py
@@ -207,7 +207,7 @@
     def send_side_rows(level):
         for side, targets in ((1, far[level]), (0, near)):
             for to in targets:
-                if level < 2 and to[3] == 1:
+                if level != 2 and to[3] == 1:
                     continue
                 if level < 3:
                     copy = send(own[level].at[0:16, W:], gat[level].at[side, mine_rows, W:], to)
@@ -279,7 +279,7 @@
         w_high, w_low = split(weights.T)
         size = 512
         for c in range(ROWS // size):
-            if c == 2:
+            if c == 3:
                 between()
             rows = pl.ds(c * size, size)
             wide = [a_buf[i, rows, :] for i in sources]
@@ -294,7 +294,7 @@
     core_rows = pl.ds(pl.multiple_of(core * 64, 64), 64)
     forward = [[], []]
     forward_late = [[], []]
-    coef_forward = [[], []]
+    coef_forward = [[], [], []]
 
     def forward_side_rows(level):
         receive(others[level])
@@ -314,7 +314,7 @@
 
     def send_coefficients(level):
         for to in near:
-            if level < 2 and to[3] == 1:
+            if to[3] == 1:
                 continue
             spread[level].append(send(us[level].at[mine], us[level].at[mine], to))
 
@@ -378,6 +378,7 @@
         forward_side_rows(1)
         advance(0, 48, 80, rests)
         send_partner(1, 32, 64, rests)
+        send_coefficients(0)
 
     inv = solve_pivots(1, late_rows)
     inv_buf[...] = inv
@@ -388,11 +389,10 @@
     send_side_rows(2)
     send_partner(2, 16, 32, nexts)
     send_partner(2, 32, 48, rests)
-    send_coefficients(0)
     send_coefficients(1)
+    forward_coefficients(0)
     inv_buf[...] = solve_pivots(2)
     receive(others[2])
-    forward_coefficients(0)
     forward_coefficients(1)
     advance_pivots(2)
     advance(2, 32, 48, rests)
@@ -405,14 +405,22 @@
     u3 = jnp.concatenate([blocks(1, b) for b in range(3)], axis=0)
     u4 = jnp.concatenate([blocks(0, b) for b in range(1, 4)], axis=0) - dot(u3, blocks(0, 0))
     apply((2, 3, 4), (0, 1), jnp.concatenate([u4, u3], axis=1), last_sends)
-    for copy in started[:-22]:
+    for copy in started[:-10]:
         copy.wait_send()
-    del started[:-22]
-    inv = solve_pivots(3)
-    receive(others[3])
+    del started[:-10]
+    last_forward = []
+
+    def forward_last():
+        receive(others[3])
+        both = gatx.at[:, core_rows, :]
+        last_forward.append(send(both, both, (z, x, 0, 1)))
+        forward_coefficients(2)
+
+    inv = solve_pivots(3, forward_last)
+    receive(last_forward)
     y_one = dot(gatx[1] - dot(gatx[0], gat[3][1]), inv)
 
-    receive(spread[2])
+    receive(coef_forward[2])
     y_two = blocks(2, 1) - dot(y_one, blocks(2, 0))
     w_high, w_low = split(jnp.concatenate([y_two.T, y_one.T], axis=0))
     w_both = jnp.concatenate([w_high, w_low], axis=1)
@@ -430,7 +438,7 @@
     f32 = jnp.float32
     hbm = pl.BlockSpec(memory_space=pl.ANY)
     pieces, widths = (16, 16, 16, 32), (384, 512, 512, 512)
-    n_copies = 7 + 4 + 12 + 4 * 15 + 2 * 9 + 2 * 15 + 7 + 2 * 4 + 7
+    n_copies = 7 + 4 + 12 + 4 * 15 + 2 * 9 + 15 + 8 + 7 + 3 * 4
     return pl.pallas_call(
         solve_kernel,
         out_shape=jax.ShapeDtypeStruct((ROWS, W), f32),

time: 58.1 us -> 59.1 us (1.017)
  Pallas kernels: 56.7 us -> 57.7 us
    pallas_call x1, Pallas kernels: 56.7 us -> 57.7 us  [body(): pl.pallas_call(solve_kernel, out_shape=jax.ShapeDtypeStruct((ROWS, W), f3...]
where the time goes in v6:
time: 59.1 us; the launch traced here: 59 us
  Pallas kernels  57.7 us (98%)
  local copies, waits for them, and re-layouts  1.32 us (2%)
    pallas_call x1, Pallas kernels, body(): pl.pallas_call(solve_kernel, out_shape=jax.ShapeDtypeStruct((ROWS, W), f3...  57.7 us
    unnamed x1, local copies, waits for them, and re-layouts  1.32 us

profile of v6, /device:TPU:1, one launch (start us, length us, event | category | flops | bytes accessed | tf_op | source)
XLA Modules:
  0.0 59.0 jit_solution(14635712449576514065)
XLA Ops:
  0.0 57.7 %solve.1 = f32[4096,128]{1,0:T(8,128)S(1)} custom-call(f32[4096,128]{1,0:T(8,128)} %l4.1, f32[4096,128]{1,0:T(8,128)} %l3.1, f32[4096,128]{1,0:T(8,128)} %l2.1, f32[4096,128]{1,0:T(8,128)} %l1.1, f32[4096,128]{1,0:T(8,128)} %x_in.1, f32[4096,128]{1,0:T(8,128)} %r4.1, f32[4096,128]{1,0:T(8,128)} %r3.1, f32[4096,128]{1,0:T(8,128)} %r2.1, f32[4096,128]{1,0:T(8,128)} %r1.1), custom_call_target="tpu_custom_call" | custom-call | tf_op jit(solution)/shard_map/solve/pallas_call | solution.py:442
  57.7 1.3 %copy.11 = f32[4096,128]{1,0:T(8,128)} copy(f32[4096,128]{1,0:T(8,128)S(1)} %solve.1) | data formatting | bytes 4194304
